TPU v7x, 512 devices: a whole 4x4x16 slice. The times are simulated.
512 devices in a mesh: lev: 32 (over x_lo, z), mem: 16 (over x_hi, y, core).
Axes of the slice: x: 4 (x_hi: 2, x_lo: 2; x = x_hi * 2 + x_lo), y: 4, z: 16, core: 2. Of those that a mesh axis runs over, the one named last changes fastest.
Arguments:
- control: bfloat16 [32, 5, 128, 4096], P('mem', None, 'lev'), may hold values from -6 to 6
- static_control_vector: bfloat16 [5, 128, 4096], P(None, None, 'lev'), may hold values from -6 to 6
- perturb: bfloat16 [32, 5, 128, 4096], P('mem', None, None, 'lev'), may hold values from -6 to 6
- tiles: bfloat16 [4, 64, 64], replicated, may hold values from -0.375 to 0.375
- block_offset: int32 [64, 4], replicated, may hold values from -8 to 8
- vert: bfloat16 [5, 128, 128], replicated, may hold values from -0.5 to 0.5
- static_vertical_root: bfloat16 [5, 128, 128], replicated, may hold values from -0.5 to 0.5
- obs_index: int32 [524288], P(('lev', 'mem')), may hold values from 0 to 5119
- obs_value: float32 [524288], P(('lev', 'mem')), may hold values from -6 to 6
- obs_sigma: float32 [524288], P(('lev', 'mem')), may hold values from 0.3 to 1
- huber_mask: int32 [524288], P(('lev', 'mem')), may hold values 0 or 1
Outputs:
- control_out: bfloat16 [32, 5, 128, 4096], P('mem', None, 'lev')
- static_out: bfloat16 [5, 128, 4096], P(None, None, 'lev')
Inputs may be any that keep to these rules, and one draw needn't show every extreme that they name: `obs_index`: indices count in the block held by the observation's own device: 5 variables, 128 / 16 levels, 128 columns, in that order. `block_offset`: source blocks wrap around the window.
All inputs are finite; a program needn't handle non-finite values. No bound on the sum of `huber_mask` on one device may be relied on, other than what follows from the above.
Results may differ from a plain program's by a relative error of at most 0.0057.
Values may be sent and summed in bfloat16 or wider, within the bound.
No kernel may reach another device: no remote copies, remote signals or barrier semaphores. Data moves between devices by JAX's collectives and lax.ppermute only.
A program may use at most 64 MiB of HBM per device.

v0:
```python
import math
import jax
import jax.numpy as jnp
from jax import lax
from jax.sharding import PartitionSpec as P

ITERS = 2
ENS_W = 0.85
STATIC_WEIGHT = 0.5
TAU = 0.5
HUBER_LOW = 0.3


def selectors(block_offset):
    count = block_offset.shape[0]
    blocks = jnp.arange(count, dtype=jnp.int32)
    source = (blocks[:, None] + block_offset) % count
    return (source.T[:, :, None] == blocks[None, None, :]).astype(jnp.bfloat16)


def horizontal(field, tiles, picks):
    count = picks.shape[1]
    width = tiles.shape[1]
    shaped = field.reshape(field.shape[:-1] + (count, width))
    total = None
    for slot in range(tiles.shape[0]):
        moved = jnp.einsum(
            "bj,...jc->...bc", picks[slot], shaped, preferred_element_type=jnp.float32
        ).astype(jnp.bfloat16)
        term = jnp.einsum("...bc,cd->...bd", moved, tiles[slot], preferred_element_type=jnp.float32)
        total = term if total is None else total + term
    return total.reshape(field.shape).astype(jnp.bfloat16)


def horizontal_adjoint(field, tiles, picks):
    count = picks.shape[1]
    width = tiles.shape[1]
    shaped = field.reshape(field.shape[:-1] + (count, width))
    total = None
    for slot in range(tiles.shape[0]):
        term = jnp.einsum(
            "...bc,dc->...bd", shaped, tiles[slot], preferred_element_type=jnp.float32
        )
        moved = jnp.einsum(
            "bj,...bd->...jd",
            picks[slot].astype(jnp.float32),
            term,
            precision=lax.Precision.HIGHEST,
        )
        total = moved if total is None else total + moved
    return total.reshape(field.shape)


def observe(block, obs_index, obs_value, precision_obs):
    flat = block.reshape(-1)
    seen = flat[obs_index]
    resid = precision_obs * (seen - obs_value)
    return jnp.zeros_like(flat).at[obs_index].add(resid).reshape(block.shape)


def on_device(
    control,
    static_control_vector,
    perturb,
    tiles,
    block_offset,
    vert,
    static_vertical_root,
    obs_index,
    obs_value,
    obs_sigma,
    huber_mask,
):
    picks = selectors(block_offset)
    members_all = control.shape[0] * lax.axis_size("mem")
    ens_gain = ENS_W / math.sqrt(members_all)
    level_rows = static_control_vector.shape[1] // lax.axis_size("mem")
    first_level = lax.axis_index("mem") * level_rows
    weights = jnp.where(huber_mask == 1, jnp.float32(1.0), jnp.float32(HUBER_LOW))
    precision_obs = weights / (obs_sigma * obs_sigma)
    vertical_forward = vert.astype(jnp.float32)
    static_forward = static_vertical_root.astype(jnp.float32)
    for turn in range(ITERS):
        local = horizontal(control, tiles, picks)
        columns = lax.all_to_all(local, "lev", split_axis=3, concat_axis=2, tiled=True)
        vertical = jnp.einsum("vlk,mvkc->mvlc", vert, columns, preferred_element_type=jnp.float32)
        partial_value = jnp.sum(vertical * perturb.astype(jnp.float32), axis=0)
        static_portion = jnp.einsum(
            "tbu,tuo->tbo",
            static_vertical_root,
            static_control_vector,
            preferred_element_type=jnp.float32,
        )
        ens = lax.psum(partial_value, "mem")
        increment = ens_gain * ens + STATIC_WEIGHT * static_portion
        own_block = lax.dynamic_slice_in_dim(increment, first_level, level_rows, 1)
        grad_block = observe(own_block, obs_index, obs_value, precision_obs)
        placed = lax.dynamic_update_slice_in_dim(
            jnp.zeros_like(increment), grad_block, first_level, 1
        )
        gradient_field_total = lax.psum(placed, "mem")
        static_gradient = static_control_vector.astype(jnp.float32) + STATIC_WEIGHT * jnp.einsum(
            "otn,ote->one", static_forward, gradient_field_total, precision=lax.Precision.HIGHEST
        )
        weighted_innovations = (ens_gain * gradient_field_total)[None] * perturb.astype(jnp.float32)
        backward_field = jnp.einsum(
            "vkl,mvkc->mvlc",
            vertical_forward,
            weighted_innovations,
            precision=lax.Precision.HIGHEST,
        ).astype(jnp.bfloat16)
        levels = lax.all_to_all(backward_field, "lev", split_axis=2, concat_axis=3, tiled=True)
        adjoint = horizontal_adjoint(levels, tiles, picks)
        current = control.astype(jnp.float32)
        control = (current - TAU * (current + adjoint)).astype(jnp.bfloat16)
        static_control_vector = (
            static_control_vector.astype(jnp.float32) - TAU * static_gradient
        ).astype(jnp.bfloat16)
    return (control, static_control_vector)


def solution(mesh):
    placed = (
        P("mem", None, "lev", None),
        P(None, None, "lev"),
        P("mem", None, None, "lev"),
        P(),
        P(),
        P(),
        P(),
        P(("lev", "mem")),
        P(("lev", "mem")),
        P(("lev", "mem")),
        P(("lev", "mem")),
    )
    return jax.shard_map(
        on_device,
        mesh=mesh,
        in_specs=placed,
        out_specs=(P("mem", None, "lev", None), P(None, None, "lev")),
        check_vma=False,
    )
```

profile of v0, /device:TPU:4, one launch (start us, length us, event | category | flops | bytes accessed | tf_op | source)
XLA Modules:
  0.0 919.5 jit_solution(7885680321525011483)
XLA Ops:
  8.0 1.6 reshape.43
  9.6 1.2 fusion.5
  12.5 9.9 %copy.161 = bf16[2,5,4,64,64]{1,2,0,4,3:T(4,128)(2,1)} copy(bf16[2,5,4,64,64]{4,3,2,1,0:T(8,128)(2,1)S(1)} %fusion.2) | data formatting | bytes 655360 | tf_op jit(solution)/shard_map/convert_element_type | solution.py:32
  22.3 13.3 %reshape.102 = bf16[32,2,2560]{2,1,0:T(2,128)(2,1)} reshape(bf16[4096,2,4,5]{3,2,1,0:T(4,128)(2,1)} %bitcast.255) | data formatting | bytes 655360
  35.6 16.1 %all-to-all-start = ((bf16[32,2,2560]{2,1,0:T(2,128)(2,1)}), bf16[32,2,2560]{2,1,0:T(2,128)(2,1)S(1)}, u32[]{:S(2)}, u32[]{:S(2)}) async-start(bf16[32,2,2560]{2,1,0:T(2,128)(2,1)} %reshape.102), calls=%async_computation | async-start | bytes 655360 | tf_op jit(solution)/shard_map/all_to_all | solution.py:85
  52.0 24.5 %all-to-all-done = bf16[32,2,2560]{2,1,0:T(2,128)(2,1)S(1)} async-done(((bf16[32,2,2560]{2,1,0:T(2,128)(2,1)}), bf16[32,2,2560]{2,1,0:T(2,128)(2,1)S(1)}, u32[]{:S(2)}, u32[]{:S(2)}) %all-to-all-start) | async-done | bytes 327712 | tf_op jit(solution)/shard_map/all_to_all | solution.py:85
  76.5 19.2 %reshape.103 = bf16[4096,2,4,5]{3,2,1,0:T(4,128)(2,1)} reshape(bf16[32,2,2560]{2,1,0:T(2,128)(2,1)S(1)} %all-to-all-done) | data formatting | bytes 655360
  95.7 11.4 %copy.89 = bf16[2,5,4,32,128]{4,2,3,1,0:T(4,128)(2,1)S(1)} copy(bf16[2,5,4,32,128]{1,2,0,4,3:T(4,128)(2,1)} %bitcast.256) | data formatting | bytes 655360 | tf_op jit(solution)/shard_map/all_to_all | solution.py:85
  107.5 0.9 copy.92
  108.7 143.3 %all-reduce.5.cloned.1.call-done = f32[5,128,128]{2,1,0:T(8,128)} async-done(((f32[5,128,128]{2,1,0:T(8,128)}), f32[5,128,128]{2,1,0:T(8,128)}) %all-reduce.5.cloned.1.call-update) | async-done | bytes 327696 | tf_op jit(solution)/shard_map/psum | solution.py:94
  252.7 6.2 gather_fusion
  258.9 5.9 scatter_custom_fusion
  265.7 151.5 %all-reduce.7.cloned.1.call-done = f32[5,128,128]{2,1,0:T(8,128)} async-done(((f32[5,128,128]{2,1,0:T(8,128)}), f32[5,128,128]{2,1,0:T(8,128)}) %all-reduce.7.cloned.1.call-update) | async-done | bytes 327696 | tf_op jit(solution)/shard_map/psum | solution.py:101
  417.2 1.0 broadcast_multiply_fusion
  418.8 0.8 copy.95
  419.6 36.8 %all_to_all.66 = bf16[2,5,128,128]{3,0,1,2:T(2,128)(2,1)S(1)} all-to-all(bf16[2,5,128,128]{3,0,1,2:T(2,128)(2,1)S(1)} %copy.95), channel_id=1, replica_groups=mesh['lev'=32,'mem'=16] {'lev'}, dimensions={2} | all-to-all | bytes 655360 | tf_op jit(solution)/shard_map/all_to_all | solution.py:112
  456.8 0.7 fusion.49
  457.6 0.8 fusion.67
  458.3 0.8 fusion.61
  459.1 0.7 fusion.55
  459.8 0.8 fusion.93
  462.1 1.8 fusion.1
  463.9 1.7 copy.102
  468.1 1.8 convolution_add_fusion.2
  469.8 2.0 convolution_add_fusion.1
  471.9 1.6 fusion.3
  473.4 11.7 %copy.163 = bf16[2,5,4,64,64]{1,2,0,4,3:T(4,128)(2,1)} copy(bf16[2,5,4,64,64]{4,3,2,1,0:T(8,128)(2,1)} %fusion.3) | data formatting | bytes 655360 | tf_op jit(solution)/shard_map/convert_element_type | solution.py:32
  485.1 13.2 %reshape.104 = bf16[32,2,2560]{2,1,0:T(2,128)(2,1)} reshape(bf16[4096,2,4,5]{3,2,1,0:T(4,128)(2,1)} %bitcast.257) | data formatting | bytes 655360
  498.3 3.9 all-to-all-start.2
  502.7 21.9 %all-to-all-done.2 = bf16[32,2,2560]{2,1,0:T(2,128)(2,1)S(1)} async-done(((bf16[32,2,2560]{2,1,0:T(2,128)(2,1)}), bf16[32,2,2560]{2,1,0:T(2,128)(2,1)S(1)}, u32[]{:S(2)}, u32[]{:S(2)}) %all-to-all-start.2) | async-done | bytes 327712 | tf_op jit(solution)/shard_map/all_to_all | solution.py:85
  524.5 19.2 %reshape.105 = bf16[4096,2,4,5]{3,2,1,0:T(4,128)(2,1)} reshape(bf16[32,2,2560]{2,1,0:T(2,128)(2,1)S(1)} %all-to-all-done.2) | data formatting | bytes 655360
  543.7 11.4 %copy.112 = bf16[2,5,4,32,128]{4,2,3,1,0:T(4,128)(2,1)S(1)} copy(bf16[2,5,4,32,128]{1,2,0,4,3:T(4,128)(2,1)} %bitcast.258) | data formatting | bytes 655360 | tf_op jit(solution)/shard_map/all_to_all | solution.py:85
  555.5 0.9 copy.114
  557.1 142.3 %all-reduce.9.cloned.1.call-done = f32[5,128,128]{2,1,0:T(8,128)} async-done(((f32[5,128,128]{2,1,0:T(8,128)}), f32[5,128,128]{2,1,0:T(8,128)}) %all-reduce.9.cloned.1.call-update) | async-done | bytes 327696 | tf_op jit(solution)/shard_map/psum | solution.py:94
  700.2 6.1 gather_fusion.1
  706.3 6.1 scatter_custom_fusion.1
  713.2 151.5 %all-reduce.11.cloned.1.call-done = f32[5,128,128]{2,1,0:T(8,128)} async-done(((f32[5,128,128]{2,1,0:T(8,128)}), f32[5,128,128]{2,1,0:T(8,128)}) %all-reduce.11.cloned.1.call-update) | async-done | bytes 327696 | tf_op jit(solution)/shard_map/psum | solution.py:101
  864.7 1.0 broadcast_multiply_fusion.1
  866.4 1.3 copy.120
  867.6 13.5 %all-to-all-start.3 = ((bf16[2,5,128,128]{3,0,1,2:T(2,128)(2,1)}), bf16[2,5,128,128]{3,0,1,2:T(2,128)(2,1)S(1)}, u32[]{:S(2)}, u32[]{:S(2)}) async-start(bf16[2,5,128,128]{3,0,1,2:T(2,128)(2,1)} %copy.120), calls=%async_computation.3 | async-start | bytes 655360 | tf_op jit(solution)/shard_map/all_to_all | solution.py:112
  881.6 0.8 copy.130
  882.4 22.2 %all-to-all-done.3 = bf16[2,5,128,128]{3,0,1,2:T(2,128)(2,1)S(1)} async-done(((bf16[2,5,128,128]{3,0,1,2:T(2,128)(2,1)}), bf16[2,5,128,128]{3,0,1,2:T(2,128)(2,1)S(1)}, u32[]{:S(2)}, u32[]{:S(2)}) %all-to-all-start.3) | async-done | bytes 327712 | tf_op jit(solution)/shard_map/all_to_all | solution.py:112
  905.1 0.7 fusion.46
  905.8 0.8 fusion.64
  906.6 0.8 fusion.58
  907.3 0.7 fusion.52
  908.1 0.8 fusion.92
  912.0 1.0 fusion.34
  (81 shorter events, 17.3 us)
Async XLA Ops:
  7.2 100.0 %copy-start = (bf16[5,128,128]{2,1,0:T(8,128)(2,1)S(1)}, bf16[5,128,128]{2,1,0:T(8,128)(2,1)}, u32[]{:S(2)}) copy-start(bf16[5,128,128]{2,1,0:T(8,128)(2,1)} %param.16) | copy-start | bytes 491524
  8.0 2.8 copy-start.7
  22.3 29.4 %copy-start.9 = (bf16[2,5,128,128]{3,2,1,0:T(8,128)(2,1)S(1)}, bf16[2,5,128,128]{3,2,1,0:T(8,128)(2,1)}, u32[]{:S(2)}) copy-start(bf16[2,5,128,128]{3,2,1,0:T(8,128)(2,1)} %param.13) | copy-start | bytes 983044
  35.6 40.9 %all-to-all-start = ((bf16[32,2,2560]{2,1,0:T(2,128)(2,1)}), bf16[32,2,2560]{2,1,0:T(2,128)(2,1)S(1)}, u32[]{:S(2)}, u32[]{:S(2)}) async-start(bf16[32,2,2560]{2,1,0:T(2,128)(2,1)} %reshape.102), calls=%async_computation | async-start | bytes 655360 | tf_op jit(solution)/shard_map/all_to_all | solution.py:85
  51.7 200.2 %all-reduce.5.cloned.1.call-start = ((), (), s32[]{:S(2)}) async-start(), calls=%async_computation.4 | async-start | bytes 655360 | tf_op jit(solution)/shard_map/psum | solution.py:94
  107.1 1.3 copy-start.13
  107.1 1.4 copy-start.1
  107.1 1.4 copy-start.8
  108.4 308.8 %all-reduce.7.cloned.1.call-start = ((), (), s32[]{:S(2)}) async-start(), calls=%async_computation.5 | async-start | bytes 655360 | tf_op jit(solution)/shard_map/psum | solution.py:101
  108.5 150.5 %copy-start.14 = (s32[1024]{0:T(1024)}, s32[1024]{0:T(1024)S(1)}, u32[]{:S(2)}) copy-start(s32[1024]{0:T(1024)S(1)} %get-tuple-element.11) | copy-start | bytes 12292
  252.7 6.2 copy-start.10
  252.7 6.2 copy-start.11
  252.7 6.2 copy-start.12
  264.9 0.7 copy-start.6
  465.6 1.0 copy-start.4
  498.3 26.2 %all-to-all-start.2 = ((bf16[32,2,2560]{2,1,0:T(2,128)(2,1)}), bf16[32,2,2560]{2,1,0:T(2,128)(2,1)S(1)}, u32[]{:S(2)}, u32[]{:S(2)}) async-start(bf16[32,2,2560]{2,1,0:T(2,128)(2,1)} %reshape.104), calls=%async_computation.2 | async-start | bytes 655360 | tf_op jit(solution)/shard_map/all_to_all | solution.py:85
  502.2 197.2 %all-reduce.9.cloned.1.call-start = ((), (), s32[]{:S(2)}) async-start(), calls=%async_computation.6 | async-start | bytes 655360 | tf_op jit(solution)/shard_map/psum | solution.py:94
  555.1 1.3 copy-start.2
  556.4 308.4 %all-reduce.11.cloned.1.call-start = ((), (), s32[]{:S(2)}) async-start(), calls=%async_computation.7 | async-start | bytes 655360 | tf_op jit(solution)/shard_map/psum | solution.py:101
  712.5 0.7 copy-start.5
  865.9 15.2 %copy-start.3 = (f32[5,128,128]{2,1,0:T(8,128)S(1)}, f32[5,128,128]{2,1,0:T(8,128)}, u32[]{:S(2)}) copy-start(f32[5,128,128]{2,1,0:T(8,128)} %all-reduce.11.cloned.1.call-done) | copy-start | bytes 983044
  867.6 37.0 %all-to-all-start.3 = ((bf16[2,5,128,128]{3,0,1,2:T(2,128)(2,1)}), bf16[2,5,128,128]{3,0,1,2:T(2,128)(2,1)S(1)}, u32[]{:S(2)}, u32[]{:S(2)}) async-start(bf16[2,5,128,128]{3,0,1,2:T(2,128)(2,1)} %copy.120), calls=%async_computation.3 | async-start | bytes 655360 | tf_op jit(solution)/shard_map/all_to_all | solution.py:112
Sparse Core Ops, SparseCore 0:
  108.5 143.3 all-reduce.4
  265.8 151.3 all-reduce.6
  556.5 142.9 all-reduce.8
  713.3 151.3 all-reduce.10
where the time goes:
time: 922 us; the launch traced here: 920 us
  waiting for transfers between devices  657 us (71%)
  local copies, waits for them, and re-layouts  135 us (15%)
  blocking collectives  36.8 us (4%)
  starting transfers between devices  33.9 us (4%)
  matrix products  24.7 us (3%)
  other arithmetic  17.5 us (2%)
  between operations  14.4 us (2%)
    psum x2, waiting for transfers between devices, on_device(): gradient_field_total = lax.psum(placed, 'mem')  303 us
    psum x2, waiting for transfers between devices, on_device(): ens = lax.psum(partial_value, 'mem')  286 us
    unnamed x37, local copies, waits for them, and re-layouts  67.9 us
    all_to_all x2, waiting for transfers between devices, on_device(): lax.all_to_all(local, 'lev', split_axis=3, concat_axis=2, tiled=True)  46.4 us
    all_to_all x1, blocking collectives, on_device(): lax.all_to_all(backward_field, 'lev', split_axis=2, concat_axis=3, tiled=...  36.8 us
    all_to_all x2, local copies, waits for them, and re-layouts, on_device(): lax.all_to_all(local, 'lev', split_axis=3, concat_axis=2, tiled=True)  22.9 us
    all_to_all x1, waiting for transfers between devices, on_device(): lax.all_to_all(backward_field, 'lev', split_axis=2, concat_axis=3, tiled=...  22.2 us
    convert_element_type x2, local copies, waits for them, and re-layouts, horizontal(): return total.reshape(field.shape).astype(jnp.bfloat16)  21.5 us
  transfers between devices with their start and end apart: 7, of which 7 were waited for; matrix products, arithmetic and copies ran while one was open for 0% of the time, Pallas kernels for 0%

commit v1 on v0

--- a/solution.py
+++ b/solution.py
@@ -91,7 +91,7 @@
             static_control_vector,
             preferred_element_type=jnp.float32,
         )
-        ens = lax.psum(partial_value, "mem")
+        ens = jnp.sum(lax.all_gather(partial_value, "mem"), axis=0)
         increment = ens_gain * ens + STATIC_WEIGHT * static_portion
         own_block = lax.dynamic_slice_in_dim(increment, first_level, level_rows, 1)
         grad_block = observe(own_block, obs_index, obs_value, precision_obs)

time: 922 us -> 767 us (0.83)
  waiting for transfers between devices: 657 us -> 477 us
  blocking collectives: 36.8 us -> 63.2 us
    psum x2 -> x0, waiting for transfers between devices: 286 us -> none  [on_device(): ens = lax.psum(partial_value, 'mem')]
    all_gather x0 -> x2, waiting for transfers between devices: none -> 126 us  [on_device(): ens = jnp.sum(lax.all_gather(partial_value, 'mem'), axis=0)]
    all_to_all x0 -> x1, blocking collectives: none -> 26.4 us  [on_device(): lax.all_to_all(local, 'lev', split_axis=3, concat_axis=2, tiled=True)]
    all_to_all x2 -> x1, waiting for transfers between devices: 46.4 us -> 24.5 us  [on_device(): lax.all_to_all(local, 'lev', split_axis=3, concat_axis=2, tiled=True)]
    all_to_all x2 -> x1, starting transfers between devices: 20 us -> 16.1 us  [on_device(): lax.all_to_all(local, 'lev', split_axis=3, concat_axis=2, tiled=True)]
  transfers between devices with their start and end apart: 7 -> 6, of which waited for: 7 -> 6; matrix products, arithmetic and copies ran while one was open for 0% -> 0% of each run, Pallas kernels for 0% -> 0%
where the time goes in v1:
time: 767 us; the launch traced here: 765 us
  waiting for transfers between devices  477 us (62%)
  local copies, waits for them, and re-layouts  134 us (17%)
  blocking collectives  63.2 us (8%)
  starting transfers between devices  30 us (4%)
  matrix products  24.7 us (3%)
  other arithmetic  21.6 us (3%)
  between operations  14.4 us (2%)
    psum x2, waiting for transfers between devices, on_device(): gradient_field_total = lax.psum(placed, 'mem')  303 us
    all_gather x2, waiting for transfers between devices, on_device(): ens = jnp.sum(lax.all_gather(partial_value, 'mem'), axis=0)  126 us
    unnamed x37, local copies, waits for them, and re-layouts  67.3 us
    all_to_all x1, blocking collectives, on_device(): lax.all_to_all(backward_field, 'lev', split_axis=2, concat_axis=3, tiled=...  36.8 us
    all_to_all x1, blocking collectives, on_device(): lax.all_to_all(local, 'lev', split_axis=3, concat_axis=2, tiled=True)  26.4 us
    all_to_all x1, waiting for transfers between devices, on_device(): lax.all_to_all(local, 'lev', split_axis=3, concat_axis=2, tiled=True)  24.5 us
    all_to_all x2, local copies, waits for them, and re-layouts, on_device(): lax.all_to_all(local, 'lev', split_axis=3, concat_axis=2, tiled=True)  22.9 us
    all_to_all x1, waiting for transfers between devices, on_device(): lax.all_to_all(backward_field, 'lev', split_axis=2, concat_axis=3, tiled=...  22 us
  transfers between devices with their start and end apart: 6, of which 6 were waited for; matrix products, arithmetic and copies ran while one was open for 0% of the time, Pallas kernels for 0%

profile of v1, /device:TPU:4, one launch (start us, length us, event | category | flops | bytes accessed | tf_op | source)
XLA Modules:
  0.0 764.6 jit_solution(12906240993579865085)
XLA Ops:
  8.0 1.6 reshape.43
  9.6 1.2 fusion.5
  12.5 9.8 %copy.161 = bf16[2,5,4,64,64]{1,2,0,4,3:T(4,128)(2,1)} copy(bf16[2,5,4,64,64]{4,3,2,1,0:T(8,128)(2,1)S(1)} %fusion.2) | data formatting | bytes 655360 | tf_op jit(solution)/shard_map/convert_element_type | solution.py:32
  22.3 13.3 %reshape.104 = bf16[32,2,2560]{2,1,0:T(2,128)(2,1)} reshape(bf16[4096,2,4,5]{3,2,1,0:T(4,128)(2,1)} %bitcast.257) | data formatting | bytes 655360
  35.6 16.1 %all-to-all-start = ((bf16[32,2,2560]{2,1,0:T(2,128)(2,1)}), bf16[32,2,2560]{2,1,0:T(2,128)(2,1)S(1)}, u32[]{:S(2)}, u32[]{:S(2)}) async-start(bf16[32,2,2560]{2,1,0:T(2,128)(2,1)} %reshape.104), calls=%async_computation | async-start | bytes 655360 | tf_op jit(solution)/shard_map/all_to_all | solution.py:85
  51.9 24.5 %all-to-all-done = bf16[32,2,2560]{2,1,0:T(2,128)(2,1)S(1)} async-done(((bf16[32,2,2560]{2,1,0:T(2,128)(2,1)}), bf16[32,2,2560]{2,1,0:T(2,128)(2,1)S(1)}, u32[]{:S(2)}, u32[]{:S(2)}) %all-to-all-start) | async-done | bytes 327712 | tf_op jit(solution)/shard_map/all_to_all | solution.py:85
  76.5 19.1 %reshape.105 = bf16[4096,2,4,5]{3,2,1,0:T(4,128)(2,1)} reshape(bf16[32,2,2560]{2,1,0:T(2,128)(2,1)S(1)} %all-to-all-done) | data formatting | bytes 655360
  95.6 11.4 %copy.89 = bf16[2,5,4,32,128]{4,2,3,1,0:T(4,128)(2,1)S(1)} copy(bf16[2,5,4,32,128]{1,2,0,4,3:T(4,128)(2,1)} %bitcast.258) | data formatting | bytes 655360 | tf_op jit(solution)/shard_map/all_to_all | solution.py:85
  107.4 0.9 copy.92
  108.6 64.0 %all-gather.5.cloned.1.call-done = f32[80,128,128]{2,1,0:T(8,128)} async-done(((f32[5,128,128]{2,1,0:T(8,128)}), f32[80,128,128]{2,1,0:T(8,128)}) %all-gather.5.cloned.1.call-update) | async-done | bytes 5242896 | tf_op jit(solution)/shard_map/all_gather | solution.py:94
  172.6 2.8 reduce_sum.37
  175.5 6.2 gather_fusion
  181.7 5.9 scatter_custom_fusion
  188.5 151.7 %all-reduce.3.cloned.1.call-done = f32[5,128,128]{2,1,0:T(8,128)} async-done(((f32[5,128,128]{2,1,0:T(8,128)}), f32[5,128,128]{2,1,0:T(8,128)}) %all-reduce.3.cloned.1.call-update) | async-done | bytes 327696 | tf_op jit(solution)/shard_map/psum | solution.py:101
  340.2 1.0 broadcast_multiply_fusion
  341.8 0.8 copy.95
  342.6 36.8 %all_to_all.66 = bf16[2,5,128,128]{3,0,1,2:T(2,128)(2,1)S(1)} all-to-all(bf16[2,5,128,128]{3,0,1,2:T(2,128)(2,1)S(1)} %copy.95), channel_id=1, replica_groups=mesh['lev'=32,'mem'=16] {'lev'}, dimensions={2} | all-to-all | bytes 655360 | tf_op jit(solution)/shard_map/all_to_all | solution.py:112
  379.8 0.7 fusion.49
  380.6 0.8 fusion.67
  381.3 0.8 fusion.61
  382.1 0.7 fusion.55
  382.8 0.8 fusion.93
  385.1 1.8 fusion.1
  386.9 1.7 copy.102
  391.0 1.8 convolution_add_fusion.2
  392.8 2.0 convolution_add_fusion.1
  394.8 1.6 fusion.3
  396.4 11.6 %copy.163 = bf16[2,5,4,64,64]{1,2,0,4,3:T(4,128)(2,1)} copy(bf16[2,5,4,64,64]{4,3,2,1,0:T(8,128)(2,1)} %fusion.3) | data formatting | bytes 655360 | tf_op jit(solution)/shard_map/convert_element_type | solution.py:32
  408.0 12.6 %reshape.106 = bf16[32,2,2560]{2,1,0:T(2,128)(2,1)S(1)} reshape(bf16[4096,2,4,5]{3,2,1,0:T(4,128)(2,1)} %bitcast.259) | data formatting | bytes 655360
  420.6 26.4 %all_to_all.67 = bf16[32,2,2560]{2,1,0:T(2,128)(2,1)S(1)} all-to-all(bf16[32,2,2560]{2,1,0:T(2,128)(2,1)S(1)} %reshape.106), channel_id=1, replica_groups=mesh['lev'=32,'mem'=16] {'lev'}, dimensions={0} | all-to-all | bytes 655360 | tf_op jit(solution)/shard_map/all_to_all | solution.py:85
  447.0 19.1 %reshape.107 = bf16[4096,2,4,5]{3,2,1,0:T(4,128)(2,1)} reshape(bf16[32,2,2560]{2,1,0:T(2,128)(2,1)S(1)} %all_to_all.67) | data formatting | bytes 655360
  466.2 11.4 %copy.112 = bf16[2,5,4,32,128]{4,2,3,1,0:T(4,128)(2,1)S(1)} copy(bf16[2,5,4,32,128]{1,2,0,4,3:T(4,128)(2,1)} %bitcast.260) | data formatting | bytes 655360 | tf_op jit(solution)/shard_map/all_to_all | solution.py:85
  477.9 0.9 copy.114
  479.8 62.5 %all-gather.7.cloned.1.call-done = f32[80,128,128]{2,1,0:T(8,128)} async-done(((f32[5,128,128]{2,1,0:T(8,128)}), f32[80,128,128]{2,1,0:T(8,128)}) %all-gather.7.cloned.1.call-update) | async-done | bytes 5242896 | tf_op jit(solution)/shard_map/all_gather | solution.py:94
  542.2 2.8 reduce_sum.39
  545.0 6.2 gather_fusion.1
  551.2 6.1 scatter_custom_fusion.1
  558.1 151.8 %all-reduce.5.cloned.1.call-done = f32[5,128,128]{2,1,0:T(8,128)} async-done(((f32[5,128,128]{2,1,0:T(8,128)}), f32[5,128,128]{2,1,0:T(8,128)}) %all-reduce.5.cloned.1.call-update) | async-done | bytes 327696 | tf_op jit(solution)/shard_map/psum | solution.py:101
  709.8 1.0 broadcast_multiply_fusion.1
  711.5 1.3 copy.120
  712.7 13.8 %all-to-all-start.3 = ((bf16[2,5,128,128]{3,0,1,2:T(2,128)(2,1)}), bf16[2,5,128,128]{3,0,1,2:T(2,128)(2,1)S(1)}, u32[]{:S(2)}, u32[]{:S(2)}) async-start(bf16[2,5,128,128]{3,0,1,2:T(2,128)(2,1)} %copy.120), calls=%async_computation.3 | async-start | bytes 655360 | tf_op jit(solution)/shard_map/all_to_all | solution.py:112
  727.0 0.8 copy.130
  727.8 22.0 %all-to-all-done.3 = bf16[2,5,128,128]{3,0,1,2:T(2,128)(2,1)S(1)} async-done(((bf16[2,5,128,128]{3,0,1,2:T(2,128)(2,1)}), bf16[2,5,128,128]{3,0,1,2:T(2,128)(2,1)S(1)}, u32[]{:S(2)}, u32[]{:S(2)}) %all-to-all-start.3) | async-done | bytes 327712 | tf_op jit(solution)/shard_map/all_to_all | solution.py:112
  750.9 0.8 fusion.64
  751.7 0.7 fusion.58
  752.5 0.8 fusion.52
  753.2 0.7 fusion.92
  757.1 1.0 fusion.34
  (82 shorter events, 16.4 us)
Async XLA Ops:
  7.2 99.9 %copy-start = (bf16[5,128,128]{2,1,0:T(8,128)(2,1)S(1)}, bf16[5,128,128]{2,1,0:T(8,128)(2,1)}, u32[]{:S(2)}) copy-start(bf16[5,128,128]{2,1,0:T(8,128)(2,1)} %param.16) | copy-start | bytes 491524
  8.0 2.8 copy-start.7
  22.3 29.4 %copy-start.9 = (bf16[2,5,128,128]{3,2,1,0:T(8,128)(2,1)S(1)}, bf16[2,5,128,128]{3,2,1,0:T(8,128)(2,1)}, u32[]{:S(2)}) copy-start(bf16[2,5,128,128]{3,2,1,0:T(8,128)(2,1)} %param.13) | copy-start | bytes 983044
  35.6 40.9 %all-to-all-start = ((bf16[32,2,2560]{2,1,0:T(2,128)(2,1)}), bf16[32,2,2560]{2,1,0:T(2,128)(2,1)S(1)}, u32[]{:S(2)}, u32[]{:S(2)}) async-start(bf16[32,2,2560]{2,1,0:T(2,128)(2,1)} %reshape.104), calls=%async_computation | async-start | bytes 655360 | tf_op jit(solution)/shard_map/all_to_all | solution.py:85
  51.7 121.0 %all-gather.5.cloned.1.call-start = ((), (), s32[]{:S(2)}) async-start(), calls=%async_computation.6 | async-start | bytes 5570560 | tf_op jit(solution)/shard_map/all_gather | solution.py:94
  107.1 1.3 copy-start.13
  107.1 1.3 copy-start.1
  107.1 1.3 copy-start.8
  108.3 231.9 %all-reduce.3.cloned.1.call-start = ((), (), s32[]{:S(2)}) async-start(), calls=%async_computation.4 | async-start | bytes 655360 | tf_op jit(solution)/shard_map/psum | solution.py:101
  108.4 73.3 %copy-start.14 = (s32[1024]{0:T(1024)}, s32[1024]{0:T(1024)S(1)}, u32[]{:S(2)}) copy-start(s32[1024]{0:T(1024)S(1)} %get-tuple-element.11) | copy-start | bytes 12292
  175.4 6.2 copy-start.10
  175.4 6.2 copy-start.11
  175.5 6.2 copy-start.12
  187.7 0.7 copy-start.6
  188.4 353.8 %all-gather.7.cloned.1.call-start = ((), (), s32[]{:S(2)}) async-start(), calls=%async_computation.7 | async-start | bytes 5570560 | tf_op jit(solution)/shard_map/all_gather | solution.py:94
  388.6 1.0 copy-start.4
  477.6 1.5 copy-start.2
  478.8 231.0 %all-reduce.5.cloned.1.call-start = ((), (), s32[]{:S(2)}) async-start(), calls=%async_computation.5 | async-start | bytes 655360 | tf_op jit(solution)/shard_map/psum | solution.py:101
  557.3 0.7 copy-start.5
  711.0 15.5 %copy-start.3 = (f32[5,128,128]{2,1,0:T(8,128)S(1)}, f32[5,128,128]{2,1,0:T(8,128)}, u32[]{:S(2)}) copy-start(f32[5,128,128]{2,1,0:T(8,128)} %all-reduce.5.cloned.1.call-done) | copy-start | bytes 983044
  712.7 37.0 %all-to-all-start.3 = ((bf16[2,5,128,128]{3,0,1,2:T(2,128)(2,1)}), bf16[2,5,128,128]{3,0,1,2:T(2,128)(2,1)S(1)}, u32[]{:S(2)}, u32[]{:S(2)}) async-start(bf16[2,5,128,128]{3,0,1,2:T(2,128)(2,1)} %copy.120), calls=%async_computation.3 | async-start | bytes 655360 | tf_op jit(solution)/shard_map/all_to_all | solution.py:112
Sparse Core Ops, SparseCore 0:
  108.5 64.1 all-gather.4
  188.5 151.6 all-reduce.2
  479.0 63.2 all-gather.6
  558.2 151.6 all-reduce.4
